TPU v7x, 32 devices: a whole 2x2x4 slice. The times are simulated.
32 devices in a mesh: dp: 4 (over y, x), seq: 8 (over z, core).
Axes of the slice: x: 2, y: 2, z: 4, core: 2. Of those that a mesh axis runs over, the one named last changes fastest.
Arguments:
- tokens: bfloat16 [8, 1024, 1024], P('dp', 'seq'), may hold values from -6 to 6
- lengths: int32 [8], P('dp'), may hold values from 32 to 1024, as said below
- w_query: bfloat16 [1024, 1024], P(('dp', 'seq')), may hold values from -0.1875 to 0.1875
- w_key: bfloat16 [1024, 1024], P(('dp', 'seq')), may hold values from -0.1875 to 0.1875
- w_value: bfloat16 [1024, 1024], P(('dp', 'seq')), may hold values from -0.1875 to 0.1875
- w_out: bfloat16 [1024, 1024], P(('dp', 'seq')), may hold values from -6 to 6
- w_up: bfloat16 [1024, 4096], P(('dp', 'seq')), may hold values from -0.1875 to 0.1875
- w_down: bfloat16 [4096, 1024], P(('dp', 'seq')), may hold values from -0.09375 to 0.09375
- b_query: bfloat16 [1024], P(('dp', 'seq')), may hold values from -3 to 3
- b_value: bfloat16 [1024], P(('dp', 'seq')), may hold values from -3 to 3
- b_out: bfloat16 [1024], P(('dp', 'seq')), may hold values from -3 to 3
- attn_gain: bfloat16 [1024], P(('dp', 'seq')), may hold values from 0.099609375 to 1.8984375
- attn_shift: bfloat16 [1024], P(('dp', 'seq')), may hold values from -3 to 3
- b_up: bfloat16 [4096], P(('dp', 'seq')), may hold values from -3 to 3
- b_down: bfloat16 [1024], P(('dp', 'seq')), may hold values from -3 to 3
- ffn_gain: bfloat16 [1024], P(('dp', 'seq')), may hold values from 0.099609375 to 1.8984375
- ffn_shift: bfloat16 [1024], P(('dp', 'seq')), may hold values from -3 to 3
- cotangent: bfloat16 [8, 1024, 1024], P('dp', 'seq'), may hold values from -6 to 6
Outputs:
- out_tokens: bfloat16 [8, 1024, 1024], P('dp', 'seq')
- grad_tokens: bfloat16 [8, 1024, 1024], P('dp', 'seq')
- query_grad: float32 [1024, 1024], P(('dp', 'seq'))
- key_grad: float32 [1024, 1024], P(('dp', 'seq'))
- value_grad: float32 [1024, 1024], P(('dp', 'seq'))
- outproj_grad: float32 [1024, 1024], P(('dp', 'seq'))
- upproj_grad: float32 [1024, 4096], P(('dp', 'seq'))
- downproj_grad: float32 [4096, 1024], P(('dp', 'seq'))
- querybias_grad: float32 [1024], P(('dp', 'seq'))
- valuebias_grad: float32 [1024], P(('dp', 'seq'))
- outbias_grad: float32 [1024], P(('dp', 'seq'))
- attngain_grad: float32 [1024], P(('dp', 'seq'))
- attnshift_grad: float32 [1024], P(('dp', 'seq'))
- upbias_grad: float32 [4096], P(('dp', 'seq'))
- downbias_grad: float32 [1024], P(('dp', 'seq'))
- ffngain_grad: float32 [1024], P(('dp', 'seq'))
- ffnshift_grad: float32 [1024], P(('dp', 'seq'))
Inputs may be any that keep to these rules, and one draw needn't show every extreme that they name: Positions 0 to lengths - 1 of a sequence are its valid tokens; in every draw one sequence has all 1024 valid.
All inputs are finite; a program needn't handle non-finite values.
Results may differ from a plain program's by a relative error of at most 0.025.
Values may be sent and summed in bfloat16 or wider, within the bound.
No kernel may reach another device: no remote copies, remote signals or barrier semaphores. Data moves between devices by JAX's collectives and lax.ppermute only.
A program may use at most 256 MiB of HBM per device.

v0:
```python
import jax
import jax.numpy as jnp
from jax import lax
from jax.sharding import PartitionSpec as P

HEADS = 16


score_scale = 0.125
epsilon = 1e-05
masked_score = -1e30


def layer_norm(values, gain, shift):
    average = jnp.mean(values, axis=-1, keepdims=True)
    centred = values - average
    variance = jnp.mean(centred * centred, axis=-1, keepdims=True)
    return centred * lax.rsqrt(variance + epsilon) * gain + shift


def gelu_exact(values):
    return jax.nn.gelu(values, approximate=False)


def project(values, weight):
    return jnp.einsum("srd,de->sre", values, weight, preferred_element_type=jnp.float32)


def project_back(grads, weight):
    return jnp.einsum("sre,de->srd", grads, weight, preferred_element_type=jnp.float32)


def outer_sum(values, grads):
    return jnp.einsum("srd,sre->de", values, grads, preferred_element_type=jnp.float32)


def row_total(grads):
    return jnp.sum(grads.astype(jnp.float32), axis=(0, 1))


def key_valid(lengths, first_index, key_count):
    places = first_index + jnp.arange(key_count, dtype=jnp.int32)
    return (places[None, :] < lengths[:, None])[:, None, None, :]


def local(
    tokens,
    lengths,
    w_query,
    w_key,
    w_value,
    w_out,
    w_up,
    w_down,
    b_query,
    b_value,
    b_out,
    attn_gain,
    attn_shift,
    b_up,
    b_down,
    ffn_gain,
    ffn_shift,
    cotangent,
):
    local_seqs, local_rows, model_width = tokens.shape
    head_count = HEADS
    head_size = model_width // head_count
    row_offset = lax.axis_index("seq") * local_rows
    bf_type = jnp.bfloat16
    fl_type = jnp.float32
    gathered = (
        lax.all_gather(w_query, ("dp", "seq"), axis=0, tiled=True),
        lax.all_gather(w_key, ("dp", "seq"), axis=0, tiled=True),
        lax.all_gather(w_value, ("dp", "seq"), axis=0, tiled=True),
        lax.all_gather(w_out, ("dp", "seq"), axis=0, tiled=True),
        lax.all_gather(w_up, ("dp", "seq"), axis=0, tiled=True),
        lax.all_gather(w_down, ("dp", "seq"), axis=0, tiled=True),
        lax.all_gather(b_query, ("dp", "seq"), axis=0, tiled=True),
        lax.all_gather(b_value, ("dp", "seq"), axis=0, tiled=True),
        lax.all_gather(b_out, ("dp", "seq"), axis=0, tiled=True),
        lax.all_gather(attn_gain, ("dp", "seq"), axis=0, tiled=True),
        lax.all_gather(attn_shift, ("dp", "seq"), axis=0, tiled=True),
        lax.all_gather(b_up, ("dp", "seq"), axis=0, tiled=True),
        lax.all_gather(b_down, ("dp", "seq"), axis=0, tiled=True),
        lax.all_gather(ffn_gain, ("dp", "seq"), axis=0, tiled=True),
        lax.all_gather(ffn_shift, ("dp", "seq"), axis=0, tiled=True),
    )
    full_query, full_key, full_value, full_out, full_up, full_down = gathered[:6]
    small_vectors = [item.astype(fl_type) for item in gathered[6:]]
    (
        bias_query,
        bias_value,
        bias_out,
        gain_one,
        shift_one,
        bias_up,
        bias_down,
        gain_two,
        shift_two,
    ) = small_vectors
    query = (project(tokens, full_query) + bias_query).astype(bf_type)
    key_rows = project(tokens, full_key).astype(bf_type)
    value_rows = (project(tokens, full_value) + bias_value).astype(bf_type)
    query_heads = query.reshape(local_seqs, local_rows, head_count, head_size)
    key_local = key_rows.reshape(local_seqs, local_rows, head_count, head_size)
    value_local = value_rows.reshape(local_seqs, local_rows, head_count, head_size)
    stat_shape = (local_seqs, head_count, local_rows)
    running_max = jnp.full(stat_shape, masked_score, fl_type)
    key_block = lax.all_gather(key_rows, "seq", axis=1, tiled=True)
    value_block = lax.all_gather(value_rows, "seq", axis=1, tiled=True)
    key_count = key_block.shape[1]
    key_heads = key_block.reshape(local_seqs, key_count, head_count, head_size)
    value_heads = value_block.reshape(local_seqs, key_count, head_count, head_size)
    scores = (
        jnp.einsum("sqhd,skhd->shqk", query_heads, key_heads, preferred_element_type=fl_type)
        * score_scale
    )
    keep_mask = key_valid(lengths, jnp.int32(0), key_count)
    new_max = jnp.maximum(running_max, jnp.max(jnp.where(keep_mask, scores, masked_score), axis=-1))
    exp_scores = jnp.where(keep_mask, jnp.exp(scores - new_max[..., None]), 0.0)
    running_sum = jnp.sum(exp_scores, axis=-1)
    update = jnp.einsum(
        "shqk,skhd->sqhd", exp_scores.astype(bf_type), value_heads, preferred_element_type=fl_type
    )
    context_sum = update
    final_max, final_sum, context_sum = (new_max, running_sum, context_sum)
    context_heads = context_sum / jnp.transpose(final_sum, (0, 2, 1))[..., None]
    log_sum = jnp.transpose(final_max + jnp.log(final_sum), (0, 2, 1))
    attn = context_heads.reshape(local_seqs, local_rows, model_width).astype(bf_type)
    resid = tokens.astype(fl_type) + project(attn, full_out) + bias_out
    first_f = layer_norm(resid, gain_one, shift_one)
    first = first_f.astype(bf_type)
    inner = project(first, full_up) + bias_up
    active = gelu_exact(inner).astype(bf_type)
    second = first.astype(fl_type) + project(active, full_down) + bias_down
    out_f, norm_two_pull = jax.vjp(layer_norm, second, gain_two, shift_two)
    out_tokens = out_f.astype(bf_type)
    back_weights = (
        lax.all_gather(w_query, ("dp", "seq"), axis=0, tiled=True),
        lax.all_gather(w_key, ("dp", "seq"), axis=0, tiled=True),
        lax.all_gather(w_value, ("dp", "seq"), axis=0, tiled=True),
        lax.all_gather(w_out, ("dp", "seq"), axis=0, tiled=True),
        lax.all_gather(w_up, ("dp", "seq"), axis=0, tiled=True),
        lax.all_gather(w_down, ("dp", "seq"), axis=0, tiled=True),
        lax.all_gather(b_query, ("dp", "seq"), axis=0, tiled=True),
        lax.all_gather(b_value, ("dp", "seq"), axis=0, tiled=True),
        lax.all_gather(b_out, ("dp", "seq"), axis=0, tiled=True),
        lax.all_gather(attn_gain, ("dp", "seq"), axis=0, tiled=True),
        lax.all_gather(attn_shift, ("dp", "seq"), axis=0, tiled=True),
        lax.all_gather(b_up, ("dp", "seq"), axis=0, tiled=True),
        lax.all_gather(b_down, ("dp", "seq"), axis=0, tiled=True),
        lax.all_gather(ffn_gain, ("dp", "seq"), axis=0, tiled=True),
        lax.all_gather(ffn_shift, ("dp", "seq"), axis=0, tiled=True),
    )
    back_query, back_key, back_value, back_out, back_up, back_down = back_weights[:6]
    d_second, ffngain_grad, ffnshift_grad = norm_two_pull(cotangent.astype(fl_type))
    d_outer = d_second.astype(bf_type)
    downbias_grad = row_total(d_outer)
    downproj_grad = outer_sum(active, d_outer)
    d_active = project_back(d_outer, back_down)
    gelu_value, gelu_pull = jax.vjp(gelu_exact, inner)
    d_inner = gelu_pull(d_active)[0].astype(bf_type)
    upbias_grad = row_total(d_inner)
    upproj_grad = outer_sum(first, d_inner)
    d_first = d_second + project_back(d_inner, back_up)
    norm_one_value, norm_one_pull = jax.vjp(layer_norm, resid, gain_one, shift_one)
    d_resid, attngain_grad, attnshift_grad = norm_one_pull(d_first)
    d_attnout = d_resid.astype(bf_type)
    outbias_grad = row_total(d_attnout)
    outproj_grad = outer_sum(attn, d_attnout)
    d_attn = project_back(d_attnout, back_out).astype(bf_type)
    d_attn_heads = d_attn.reshape(local_seqs, local_rows, head_count, head_size)
    row_delta = jnp.sum(d_attn_heads.astype(fl_type) * context_heads, axis=-1)
    lse_heads = jnp.transpose(log_sum, (0, 2, 1))
    delta_heads = jnp.transpose(row_delta, (0, 2, 1))
    key_block = lax.all_gather(key_rows, "seq", axis=1, tiled=True)
    value_block = lax.all_gather(value_rows, "seq", axis=1, tiled=True)
    key_count = key_block.shape[1]
    key_heads = key_block.reshape(local_seqs, key_count, head_count, head_size)
    value_heads = value_block.reshape(local_seqs, key_count, head_count, head_size)
    scores = (
        jnp.einsum("sqhd,skhd->shqk", query_heads, key_heads, preferred_element_type=fl_type)
        * score_scale
    )
    keep_mask = key_valid(lengths, jnp.int32(0), key_count)
    probs_block = jnp.where(keep_mask, jnp.exp(scores - lse_heads[..., None]), 0.0)
    d_probs = jnp.einsum(
        "sqhd,skhd->shqk", d_attn_heads, value_heads, preferred_element_type=fl_type
    )
    d_scores = (probs_block * (d_probs - delta_heads[..., None])).astype(bf_type)
    d_query_f = jnp.einsum("shqk,skhd->sqhd", d_scores, key_heads, preferred_element_type=fl_type)
    all_lse, all_delta = (
        lax.all_gather(log_sum, "seq", axis=1, tiled=True),
        lax.all_gather(row_delta, "seq", axis=1, tiled=True),
    )
    local_mask = key_valid(lengths, row_offset, local_rows)
    query_block = lax.all_gather(query, "seq", axis=1, tiled=True)
    grad_block = lax.all_gather(d_attn, "seq", axis=1, tiled=True)
    query_count = query_block.shape[1]
    remote_query = query_block.reshape(local_seqs, query_count, head_count, head_size)
    remote_grad = grad_block.reshape(local_seqs, query_count, head_count, head_size)
    remote_lse = jnp.transpose(all_lse, (0, 2, 1))
    remote_delta = jnp.transpose(all_delta, (0, 2, 1))
    scores = (
        jnp.einsum("sqhd,skhd->shqk", remote_query, key_local, preferred_element_type=fl_type)
        * score_scale
    )
    probs_block = jnp.where(local_mask, jnp.exp(scores - remote_lse[..., None]), 0.0)
    d_value_sum = jnp.einsum(
        "shqk,sqhd->skhd", probs_block.astype(bf_type), remote_grad, preferred_element_type=fl_type
    )
    d_probs = jnp.einsum(
        "sqhd,skhd->shqk", remote_grad, value_local, preferred_element_type=fl_type
    )
    d_scores = (probs_block * (d_probs - remote_delta[..., None])).astype(bf_type)
    d_key_sum = jnp.einsum(
        "shqk,sqhd->skhd", d_scores, remote_query, preferred_element_type=fl_type
    )
    flat_shape = (local_seqs, local_rows, model_width)
    d_query = (d_query_f * score_scale).reshape(flat_shape).astype(bf_type)
    d_key = (d_key_sum * score_scale).reshape(flat_shape).astype(bf_type)
    d_value = d_value_sum.reshape(flat_shape).astype(bf_type)
    querybias_grad = row_total(d_query)
    valuebias_grad = row_total(d_value)
    query_grad = outer_sum(tokens, d_query)
    key_grad = outer_sum(tokens, d_key)
    value_grad = outer_sum(tokens, d_value)
    grad_inputs = (
        d_resid
        + project_back(d_query, back_query)
        + project_back(d_key, back_key)
        + project_back(d_value, back_value)
    )
    shards = (
        lax.psum_scatter(query_grad, ("dp", "seq"), scatter_dimension=0, tiled=True),
        lax.psum_scatter(key_grad, ("dp", "seq"), scatter_dimension=0, tiled=True),
        lax.psum_scatter(value_grad, ("dp", "seq"), scatter_dimension=0, tiled=True),
        lax.psum_scatter(outproj_grad, ("dp", "seq"), scatter_dimension=0, tiled=True),
        lax.psum_scatter(upproj_grad, ("dp", "seq"), scatter_dimension=0, tiled=True),
        lax.psum_scatter(downproj_grad, ("dp", "seq"), scatter_dimension=0, tiled=True),
        lax.psum_scatter(querybias_grad, ("dp", "seq"), scatter_dimension=0, tiled=True),
        lax.psum_scatter(valuebias_grad, ("dp", "seq"), scatter_dimension=0, tiled=True),
        lax.psum_scatter(outbias_grad, ("dp", "seq"), scatter_dimension=0, tiled=True),
        lax.psum_scatter(attngain_grad, ("dp", "seq"), scatter_dimension=0, tiled=True),
        lax.psum_scatter(attnshift_grad, ("dp", "seq"), scatter_dimension=0, tiled=True),
        lax.psum_scatter(upbias_grad, ("dp", "seq"), scatter_dimension=0, tiled=True),
        lax.psum_scatter(downbias_grad, ("dp", "seq"), scatter_dimension=0, tiled=True),
        lax.psum_scatter(ffngain_grad, ("dp", "seq"), scatter_dimension=0, tiled=True),
        lax.psum_scatter(ffnshift_grad, ("dp", "seq"), scatter_dimension=0, tiled=True),
    )
    return (
        out_tokens,
        grad_inputs.astype(bf_type),
        shards[0],
        shards[1],
        shards[2],
        shards[3],
        shards[4],
        shards[5],
        shards[6],
        shards[7],
        shards[8],
        shards[9],
        shards[10],
        shards[11],
        shards[12],
        shards[13],
        shards[14],
    )


def solution(mesh):
    return jax.shard_map(
        local,
        mesh=mesh,
        in_specs=(
            P("dp", "seq", None),
            P("dp"),
            P(("dp", "seq"), None),
            P(("dp", "seq"), None),
            P(("dp", "seq"), None),
            P(("dp", "seq"), None),
            P(("dp", "seq"), None),
            P(("dp", "seq"), None),
            P(("dp", "seq")),
            P(("dp", "seq")),
            P(("dp", "seq")),
            P(("dp", "seq")),
            P(("dp", "seq")),
            P(("dp", "seq")),
            P(("dp", "seq")),
            P(("dp", "seq")),
            P(("dp", "seq")),
            P("dp", "seq", None),
        ),
        out_specs=(
            P("dp", "seq", None),
            P("dp", "seq", None),
            P(("dp", "seq"), None),
            P(("dp", "seq"), None),
            P(("dp", "seq"), None),
            P(("dp", "seq"), None),
            P(("dp", "seq"), None),
            P(("dp", "seq"), None),
            P(("dp", "seq")),
            P(("dp", "seq")),
            P(("dp", "seq")),
            P(("dp", "seq")),
            P(("dp", "seq")),
            P(("dp", "seq")),
            P(("dp", "seq")),
            P(("dp", "seq")),
            P(("dp", "seq")),
        ),
        check_vma=False,
    )
```

profile of v0, /device:TPU:0, one launch (start us, length us, event | category | flops | bytes accessed | tf_op | source)
XLA Modules:
  0.0 1550.4 jit_solution(16893591043110299912)
XLA Ops:
  9.6 60.6 %all-gather.18.cloned.1.call-done = bf16[1024,1024]{1,0:T(8,128)(2,1)} async-done(((bf16[32,1024]{1,0:T(8,128)(2,1)}), bf16[1024,1024]{1,0:T(8,128)(2,1)}) %all-gather.18.cloned.1.call-update) | async-done | bytes 2097168 | tf_op jit(solution)/shard_map/all_gather | solution.py:74
  75.5 38.9 %all-reduce.18 = (bf16[1024]{0:T(1024)(128)(2,1)S(1)}, bf16[1024]{0:T(1024)(128)(2,1)S(1)}, bf16[1024]{0:T(1024)(128)(2,1)S(1)}, bf16[1024]{0:T(1024)(128)(2,1)S...) all-reduce(bf16[1024]{0:T(1024)(128)(2,1)S(1)} %dynamic-update-slic, ...), channel_id=1, replica_groups=mesh['dp'=4,'seq'=8] {'dp','seq'}, use_global_device_ids=true, to_apply=%add | all-reduce | flops 8192 | bytes 32768
  114.3 14.2 all-gather.12.cloned.1.call-done
  133.8 39.5 %all-gather = bf16[32,1,128]{2,1,0:T(2,128)(2,1)S(1)} all-gather(bf16[1,1,128]{2,1,0:T(2,128)(2,1)S(1)} %bitcast.197), channel_id=1, replica_groups=mesh['dp'=4,'seq'=8] {'dp','seq'}, dimensions={0}, use_global_device_ids=true | all-gather | bytes 8448 | tf_op jit(solution)/shard_map/all_gather | solution.py:84
  173.4 13.4 all-gather.16.cloned.1.call-done
  190.2 44.4 %all-gather.20.cloned.1.call-done = bf16[2,1024,1024]{2,1,0:T(8,128)(2,1)} async-done(((bf16[2,128,1024]{2,1,0:T(8,128)(2,1)}), bf16[2,1024,1024]{2,1,0:T(8,128)(2,1)}) %all-gather.20.cloned.1.call-update) | async-done | bytes 4194320 | tf_op jit(solution)/shard_map/all_gather | solution.py:110
  255.1 27.2 %all-gather.14.cloned.1.call-done = bf16[2,1024,1024]{2,1,0:T(8,128)(2,1)} async-done(((bf16[2,128,1024]{2,1,0:T(8,128)(2,1)}), bf16[2,1024,1024]{2,1,0:T(8,128)(2,1)}) %all-gather.14.cloned.1.call-update) | async-done | bytes 4194320 | tf_op jit(solution)/shard_map/all_gather | solution.py:111
  288.5 11.5 fusion.129
  300.0 40.4 %all-gather.22.cloned.1.call-done = bf16[1024,1024]{1,0:T(8,128)(2,1)} async-done(((bf16[32,1024]{1,0:T(8,128)(2,1)}), bf16[1024,1024]{1,0:T(8,128)(2,1)}) %all-gather.22.cloned.1.call-update) | async-done | bytes 2097168 | tf_op jit(solution)/shard_map/all_gather | solution.py:76
  343.3 76.0 %all-gather.24.cloned.1.call-done = bf16[1024,4096]{1,0:T(8,128)(2,1)} async-done(((bf16[32,4096]{1,0:T(8,128)(2,1)}), bf16[1024,4096]{1,0:T(8,128)(2,1)}) %all-gather.24.cloned.1.call-update) | async-done | bytes 8388624 | tf_op jit(solution)/shard_map/all_gather | solution.py:77
  419.3 7.0 fusion.112
  428.4 10.8 multiply_convert_fusion.4
  439.3 58.7 %all-gather.26.cloned.1.call-done = bf16[4096,1024]{1,0:T(8,128)(2,1)} async-done(((bf16[128,1024]{1,0:T(8,128)(2,1)}), bf16[4096,1024]{1,0:T(8,128)(2,1)}) %all-gather.26.cloned.1.call-update) | async-done | bytes 8388624 | tf_op jit(solution)/shard_map/all_gather | solution.py:78
  506.5 7.5 convert_reduce_fusion
  514.0 7.1 multiply_reduce_fusion
  529.0 12.3 convert_reduce_fusion.5
  550.7 6.3 copy.76
  557.0 14.7 all_gather.89
  571.7 10.4 fusion.132
  582.1 11.2 all-gather.30.cloned.1.call-done
  599.6 9.8 convert_reduce_fusion.4
  619.5 14.1 all_gather.91
  633.5 14.0 multiply_convert_fusion.15
  658.2 9.7 convolution_bitcast_fusion.1
  669.0 9.7 convolution_bitcast_fusion
  678.9 40.1 %all-reduce.17 = (f32[1024]{0:T(1024)S(1)}, f32[1024]{0:T(1024)S(1)}, f32[1024]{0:T(1024)S(1)}, f32[1024]{0:T(1024)S(1)}, f32[1024]{0:T(1024)S(1)}, /*index=5*/f...) all-reduce(f32[1024]{0:T(1024)S(1)} %reduce_sum.191, ...), channel_id=8, replica_groups=mesh['dp'=4,'seq'=8] {'dp','seq'}, use_global_device_ids=true, to_apply=%region_18.19.clone | all-reduce | flops 12288 | bytes 98304
  729.1 9.9 reduce-scatter.13.cloned.1.call-done
  739.0 144.0 %reduce-scatter.19.cloned.1.call-done = f32[32,1024]{1,0:T(8,128)} async-done(((f32[1024,1024]{1,0:T(8,128)}), f32[32,1024]{1,0:T(8,128)}) %reduce-scatter.19.cloned.1.call-update) | async-done | bytes 131088
  883.0 143.9 %reduce-scatter.23.cloned.1.call-done = f32[32,1024]{1,0:T(8,128)} async-done(((f32[1024,1024]{1,0:T(8,128)}), f32[32,1024]{1,0:T(8,128)}) %reduce-scatter.23.cloned.1.call-update) | async-done | bytes 131088
  1026.9 143.2 %reduce-scatter.21.cloned.1.call-done = f32[32,1024]{1,0:T(8,128)} async-done(((f32[1024,1024]{1,0:T(8,128)}), f32[32,1024]{1,0:T(8,128)}) %reduce-scatter.21.cloned.1.call-update) | async-done | bytes 131088
  1170.0 186.5 %reduce-scatter.15.cloned.1.call-done = f32[32,4096]{1,0:T(8,128)} async-done(((f32[1024,4096]{1,0:T(8,128)}), f32[32,4096]{1,0:T(8,128)}) %reduce-scatter.15.cloned.1.call-update) | async-done | bytes 524304 | tf_op jit(solution)/shard_map/reduce_scatter | solution.py:240
  1356.5 187.1 %reduce-scatter.17.cloned.1.call-done = f32[128,1024]{1,0:T(8,128)} async-done(((f32[4096,1024]{1,0:T(8,128)}), f32[128,1024]{1,0:T(8,128)}) %reduce-scatter.17.cloned.1.call-update) | async-done | bytes 524304 | tf_op jit(solution)/shard_map/reduce_scatter | solution.py:241
  (182 shorter events, 111.6 us)
Async XLA Ops:
  7.2 121.3 %copy-start.3 = (bf16[2,128,1024]{2,1,0:T(8,128)(2,1)S(1)}, bf16[2,128,1024]{2,1,0:T(8,128)(2,1)}, u32[]{:S(2)}) copy-start(bf16[2,128,1024]{2,1,0:T(8,128)(2,1)} %param.18) | copy-start | bytes 1572868
  7.2 66.4 %copy-start.25 = (bf16[32]{0:T(256)(128)(2,1)S(1)}, bf16[32]{0:T(256)(128)(2,1)}, u32[]{:S(2)}) copy-start(bf16[32]{0:T(256)(128)(2,1)} %param.27) | copy-start | bytes 196
  7.2 66.6 %copy-start.26 = (bf16[32]{0:T(256)(128)(2,1)S(1)}, bf16[32]{0:T(256)(128)(2,1)}, u32[]{:S(2)}) copy-start(bf16[32]{0:T(256)(128)(2,1)} %param.26) | copy-start | bytes 196
  7.2 66.8 %copy-start.27 = (bf16[32]{0:T(256)(128)(2,1)S(1)}, bf16[32]{0:T(256)(128)(2,1)}, u32[]{:S(2)}) copy-start(bf16[32]{0:T(256)(128)(2,1)} %param.28) | copy-start | bytes 196
  7.2 67.1 %copy-start.28 = (bf16[32]{0:T(256)(128)(2,1)S(1)}, bf16[32]{0:T(256)(128)(2,1)}, u32[]{:S(2)}) copy-start(bf16[32]{0:T(256)(128)(2,1)} %param.29) | copy-start | bytes 196
  7.2 67.3 %copy-start.29 = (bf16[32]{0:T(256)(128)(2,1)S(1)}, bf16[32]{0:T(256)(128)(2,1)}, u32[]{:S(2)}) copy-start(bf16[32]{0:T(256)(128)(2,1)} %param.30) | copy-start | bytes 196
  7.3 67.5 %copy-start.30 = (bf16[32]{0:T(256)(128)(2,1)S(1)}, bf16[32]{0:T(256)(128)(2,1)}, u32[]{:S(2)}) copy-start(bf16[32]{0:T(256)(128)(2,1)} %param.32) | copy-start | bytes 196
  7.3 67.7 %copy-start.31 = (bf16[32]{0:T(256)(128)(2,1)S(1)}, bf16[32]{0:T(256)(128)(2,1)}, u32[]{:S(2)}) copy-start(bf16[32]{0:T(256)(128)(2,1)} %param.33) | copy-start | bytes 196
  7.3 68.0 %copy-start.32 = (bf16[32]{0:T(256)(128)(2,1)S(1)}, bf16[32]{0:T(256)(128)(2,1)}, u32[]{:S(2)}) copy-start(bf16[32]{0:T(256)(128)(2,1)} %param.34) | copy-start | bytes 196
  7.3 62.9 %all-gather.18.cloned.1.call-start = ((), (), s32[]{:S(2)}) async-start(), calls=%async_computation.9 | async-start | bytes 2162688 | tf_op jit(solution)/shard_map/all_gather | solution.py:74
  8.0 120.5 %all-gather.12.cloned.1.call-start = ((), (), s32[]{:S(2)}) async-start(), calls=%async_computation.6 | async-start | bytes 2162688 | tf_op jit(solution)/shard_map/all_gather | solution.py:75
  8.8 178.0 %all-gather.16.cloned.1.call-start = ((), (), s32[]{:S(2)}) async-start(), calls=%async_computation.8 | async-start | bytes 2162688 | tf_op jit(solution)/shard_map/all_gather | solution.py:73
  9.5 124.3 %copy-start.23 = (bf16[128]{0:T(256)(128)(2,1)S(1)}, bf16[128]{0:T(256)(128)(2,1)}, u32[]{:S(2)}) copy-start(bf16[128]{0:T(256)(128)(2,1)} %param.31) | copy-start | bytes 772
  9.5 163.8 %copy-start.24 = (s32[2]{0:T(128)S(1)}, s32[2]{0:T(128)}, u32[]{:S(2)}) copy-start(s32[2]{0:T(128)} %param.19) | copy-start | bytes 28
  9.5 225.0 %all-gather.20.cloned.1.call-start = ((), (), s32[]{:S(2)}) async-start(), calls=%async_computation.10 | async-start | bytes 4718592 | tf_op jit(solution)/shard_map/all_gather | solution.py:110
  73.5 208.8 %all-gather.14.cloned.1.call-start = ((), (), s32[]{:S(2)}) async-start(), calls=%async_computation.7 | async-start | bytes 4718592 | tf_op jit(solution)/shard_map/all_gather | solution.py:111
  131.6 208.7 %all-gather.22.cloned.1.call-start = ((), (), s32[]{:S(2)}) async-start(), calls=%async_computation.11 | async-start | bytes 2162688 | tf_op jit(solution)/shard_map/all_gather | solution.py:76
  132.2 287.1 %all-gather.24.cloned.1.call-start = ((), (), s32[]{:S(2)}) async-start(), calls=%async_computation.12 | async-start | bytes 8650752 | tf_op jit(solution)/shard_map/all_gather | solution.py:77
  133.0 365.0 %all-gather.26.cloned.1.call-start = ((), (), s32[]{:S(2)}) async-start(), calls=%async_computation.13 | async-start | bytes 8650752 | tf_op jit(solution)/shard_map/all_gather | solution.py:78
  133.7 416.9 %all-gather.28.cloned.1.call-start = ((), (), s32[]{:S(2)}) async-start(), calls=%async_computation.14 | async-start | bytes 4718592 | tf_op jit(solution)/shard_map/all_gather | solution.py:198
  189.9 403.4 %all-gather.30.cloned.1.call-start = ((), (), s32[]{:S(2)}) async-start(), calls=%async_computation.15 | async-start | bytes 4718592 | tf_op jit(solution)/shard_map/all_gather | solution.py:199
  300.0 126.4 %copy-start.9 = (bf16[2,128,16,64]{1,3,2,0:T(8,128)(2,1)}, bf16[2,128,16,64]{1,3,2,0:T(8,128)(2,1)S(1)}, u32[]{:S(2)}) copy-start(bf16[2,128,16,64]{1,3,2,0:T(8,128)(2,1)S(1)} %get-tuple-element.108) | copy-start | bytes 1572868
  343.3 83.0 %copy-start.11 = (bf16[2,128,1024]{2,1,0:T(8,128)(2,1)}, bf16[2,128,1024]{2,1,0:T(8,128)(2,1)S(1)}, u32[]{:S(2)}) copy-start(bf16[2,128,1024]{2,1,0:T(8,128)(2,1)S(1)} %add_convert_fusion.2) | copy-start | bytes 1572868
  439.3 64.7 %copy-start.2 = (bf16[2,128,4096]{2,1,0:T(8,128)(2,1)}, bf16[2,128,4096]{2,1,0:T(8,128)(2,1)S(1)}, u32[]{:S(2)}) copy-start(bf16[2,128,4096]{2,1,0:T(8,128)(2,1)S(1)} %get-tuple-element.101) | copy-start | bytes 6291460
  524.3 214.7 %reduce-scatter.13.cloned.1.call-start = ((), (), s32[]{:S(2)}) async-start(), calls=%async_computation.16 | async-start | bytes 4325376 | tf_op jit(solution)/shard_map/reduce_scatter | solution.py:239
  527.2 355.8 %reduce-scatter.19.cloned.1.call-start = ((), (), s32[]{:S(2)}) async-start(), calls=%async_computation.19 | async-start | bytes 4325376
  529.0 12.3 copy-start.4
  549.4 477.5 %reduce-scatter.23.cloned.1.call-start = ((), (), s32[]{:S(2)}) async-start(), calls=%async_computation.21 | async-start | bytes 4325376
  617.5 552.6 %reduce-scatter.21.cloned.1.call-start = ((), (), s32[]{:S(2)}) async-start(), calls=%async_computation.20 | async-start | bytes 4325376
  633.5 14.0 copy-start.1
  657.2 699.3 %reduce-scatter.15.cloned.1.call-start = ((), (), s32[]{:S(2)}) async-start(), calls=%async_computation.17 | async-start | bytes 17301504 | tf_op jit(solution)/shard_map/reduce_scatter | solution.py:240
  668.0 875.7 %reduce-scatter.17.cloned.1.call-start = ((), (), s32[]{:S(2)}) async-start(), calls=%async_computation.18 | async-start | bytes 17301504 | tf_op jit(solution)/shard_map/reduce_scatter | solution.py:241
  (17 other events, 63.2 us)
Sparse Core Ops, SparseCore 0:
  11.1 59.0 all-gather.17
  73.2 55.2 all-gather.11
  131.5 55.2 all-gather.15
  188.8 45.7 all-gather.19
  236.6 45.6 all-gather.13
  285.1 55.1 all-gather.21
  343.3 75.9 all-gather.23
  422.3 75.6 all-gather.25
  499.6 45.4 all-gather.27
  546.6 46.7 all-gather.29
  596.2 142.7 reduce-scatter.12
  741.7 141.2 reduce-scatter.18
  885.8 140.9 reduce-scatter.22
  1029.6 140.4 reduce-scatter.20
  1172.8 183.7 reduce-scatter.14
  1359.3 184.3 reduce-scatter.16
where the time goes:
time: 1560 us; the launch traced here: 1550 us
  waiting for transfers between devices  1160 us (74%)
  blocking collectives  147 us (9%)
  matrix products  139 us (9%)
  local copies, waits for them, and re-layouts  63.4 us (4%)
  other arithmetic  20 us (1%)
    unnamed x19, waiting for transfers between devices  435 us
    reduce_scatter x1, waiting for transfers between devices, local(): lax.psum_scatter(downproj_grad, ('dp', 'seq'), scatter_dimension=0, tiled...  187 us
    reduce_scatter x1, waiting for transfers between devices, local(): lax.psum_scatter(upproj_grad, ('dp', 'seq'), scatter_dimension=0, tiled=T...  187 us
    unnamed x2, blocking collectives  78.9 us
    all_gather x1, waiting for transfers between devices, local(): lax.all_gather(w_up, ('dp', 'seq'), axis=0, tiled=True)  76 us
    all_gather x1, waiting for transfers between devices, local(): lax.all_gather(w_key, ('dp', 'seq'), axis=0, tiled=True)  60.6 us
    all_gather x1, waiting for transfers between devices, local(): lax.all_gather(w_down, ('dp', 'seq'), axis=0, tiled=True)  58.7 us
    all_gather x1, waiting for transfers between devices, local(): key_block = lax.all_gather(key_rows, 'seq', axis=1, tiled=True)  44.4 us
  transfers between devices with their start and end apart: 16, of which 15 were waited for; matrix products, arithmetic and copies ran while one was open for 14% of the time, Pallas kernels for 0%

commit v1 on v0

--- a/solution.py
+++ b/solution.py
@@ -1,3 +1,5 @@
+import functools
+
 import jax
 import jax.numpy as jnp
 from jax import lax
@@ -43,7 +45,7 @@
     return (places[None, :] < lengths[:, None])[:, None, None, :]
 
 
-def local(
+def local_gathered(
     tokens,
     lengths,
     w_query,
@@ -270,9 +272,207 @@
     )
 
 
+BOTH = ("dp", "seq")
+SMALL_ROWS = 8
+
+
+def exchange(values, axis, split, join):
+    return lax.all_to_all(values, axis, split_axis=split, concat_axis=join, tiled=True)
+
+
+def local_heads(
+    dp_size,
+    seq_size,
+    tokens,
+    lengths,
+    w_query,
+    w_key,
+    w_value,
+    w_out,
+    w_up,
+    w_down,
+    b_query,
+    b_value,
+    b_out,
+    attn_gain,
+    attn_shift,
+    b_up,
+    b_down,
+    ffn_gain,
+    ffn_shift,
+    cotangent,
+):
+    bf_type = jnp.bfloat16
+    fl_type = jnp.float32
+    count = dp_size * seq_size
+    seqs, rows, width = tokens.shape
+    full_rows = rows * seq_size
+    own_rows = w_query.shape[0]
+    own_units = w_down.shape[0]
+    head_size = width // HEADS
+    own_heads = HEADS // seq_size
+    columns = own_heads * head_size
+    seq_at = lax.axis_index("seq")
+
+    stacked = jnp.stack((w_query, w_key, w_value), axis=1).reshape(own_rows, 3, seq_size, columns)
+    by_owner = jnp.transpose(stacked, (2, 0, 1, 3)).reshape(seq_size, own_rows, 3 * columns)
+    vectors = (b_up, b_query, b_value, b_out, attn_gain, attn_shift, b_down, ffn_gain, ffn_shift)
+    small_own = jnp.concatenate(vectors)
+    small_room = SMALL_ROWS * 3 * columns
+    small_block = jnp.pad(small_own, (0, small_room - small_own.shape[0])).reshape(SMALL_ROWS, 3 * columns)
+    payload = jnp.concatenate(
+        (by_owner, jnp.broadcast_to(small_block[None], (seq_size, SMALL_ROWS, 3 * columns))), axis=1
+    )
+    payload = jnp.broadcast_to(payload[None], (dp_size,) + payload.shape)
+    payload = payload.reshape(count, own_rows + SMALL_ROWS, 3 * columns)
+    arrived = exchange(payload, BOTH, 0, 0)
+    head_weights = arrived[:, :own_rows].reshape(width, 3 * columns)
+    small_all = arrived[:, own_rows:].reshape(count, small_room)
+    full_vectors = []
+    at = 0
+    for item in vectors:
+        size = item.shape[0]
+        full_vectors.append(small_all[:, at : at + size].reshape(count * size).astype(fl_type))
+        at += size
+    (
+        bias_up,
+        bias_query,
+        bias_value,
+        bias_out,
+        gain_one,
+        shift_one,
+        bias_down,
+        gain_two,
+        shift_two,
+    ) = full_vectors
+
+    all_tokens = lax.all_gather(tokens, "seq", axis=1, tiled=True)
+    out_up = lax.all_gather(jnp.concatenate((w_out, w_up), axis=1), BOTH, axis=0, tiled=True)
+    full_out, full_up = out_up[:, :width], out_up[:, width:]
+    full_down = lax.all_gather(w_down, BOTH, axis=0, tiled=True)
+    full_qkv = lax.all_gather(jnp.concatenate((w_query, w_key, w_value), axis=1), BOTH, axis=0, tiled=True)
+
+    own_bias = jnp.concatenate(
+        (
+            lax.dynamic_slice_in_dim(bias_query, seq_at * columns, columns),
+            jnp.zeros((columns,), fl_type),
+            lax.dynamic_slice_in_dim(bias_value, seq_at * columns, columns),
+        )
+    )
+    mixed = (project(all_tokens, head_weights) + own_bias).astype(bf_type)
+    mixed = mixed.reshape(seqs, full_rows, 3, own_heads, head_size)
+    query, keys, values = mixed[:, :, 0], mixed[:, :, 1], mixed[:, :, 2]
+    keep = key_valid(lengths, jnp.int32(0), full_rows)
+    scores = jnp.einsum("sqhd,skhd->shqk", query, keys, preferred_element_type=fl_type) * score_scale
+    row_max = jnp.max(jnp.where(keep, scores, masked_score), axis=-1)
+    exps = jnp.where(keep, jnp.exp(scores - row_max[..., None]), 0.0)
+    row_sum = jnp.sum(exps, axis=-1)
+    context = jnp.einsum("shqk,skhd->sqhd", exps.astype(bf_type), values, preferred_element_type=fl_type)
+    context = context / jnp.transpose(row_sum, (0, 2, 1))[..., None]
+    log_sum = row_max + jnp.log(row_sum)
+    attn = exchange(context.reshape(seqs, full_rows, columns).astype(bf_type), "seq", 1, 2)
+
+    resid = tokens.astype(fl_type) + project(attn, full_out) + bias_out
+    first = layer_norm(resid, gain_one, shift_one).astype(bf_type)
+    inner = project(first, full_up) + bias_up
+    active = gelu_exact(inner).astype(bf_type)
+    second = first.astype(fl_type) + project(active, full_down) + bias_down
+    out_f, norm_two_pull = jax.vjp(layer_norm, second, gain_two, shift_two)
+    out_tokens = out_f.astype(bf_type)
+
+    d_second, ffngain_grad, ffnshift_grad = norm_two_pull(cotangent.astype(fl_type))
+    d_outer = d_second.astype(bf_type)
+    downbias_grad = row_total(d_outer)
+    downproj_grad = outer_sum(active, d_outer)
+    d_active = project_back(d_outer, full_down)
+    gelu_value, gelu_pull = jax.vjp(gelu_exact, inner)
+    d_inner = gelu_pull(d_active)[0].astype(bf_type)
+    upbias_grad = row_total(d_inner)
+    upproj_grad = outer_sum(first, d_inner)
+    d_first = d_second + project_back(d_inner, full_up)
+    norm_one_value, norm_one_pull = jax.vjp(layer_norm, resid, gain_one, shift_one)
+    d_resid, attngain_grad, attnshift_grad = norm_one_pull(d_first)
+    d_attnout = d_resid.astype(bf_type)
+    outbias_grad = row_total(d_attnout)
+    outproj_grad = outer_sum(attn, d_attnout)
+    d_attn_rows = project_back(d_attnout, full_out).astype(bf_type)
+
+    down_shard = lax.psum_scatter(downproj_grad.astype(bf_type), BOTH, scatter_dimension=0, tiled=True)
+    outup_grad = jnp.concatenate((outproj_grad.astype(bf_type), upproj_grad.astype(bf_type)), axis=1)
+    outup_shard = lax.psum_scatter(outup_grad, BOTH, scatter_dimension=0, tiled=True).astype(fl_type)
+
+    d_attn = exchange(d_attn_rows, "seq", 2, 1).reshape(seqs, full_rows, own_heads, head_size)
+    delta = jnp.transpose(jnp.sum(d_attn.astype(fl_type) * context, axis=-1), (0, 2, 1))
+    scores = jnp.einsum("sqhd,skhd->shqk", query, keys, preferred_element_type=fl_type) * score_scale
+    probs = jnp.where(keep, jnp.exp(scores - log_sum[..., None]), 0.0)
+    d_probs = jnp.einsum("sqhd,skhd->shqk", d_attn, values, preferred_element_type=fl_type)
+    d_scores = (probs * (d_probs - delta[..., None])).astype(bf_type)
+    d_query = jnp.einsum("shqk,skhd->sqhd", d_scores, keys, preferred_element_type=fl_type) * score_scale
+    d_keys = jnp.einsum("shqk,sqhd->skhd", d_scores, query, preferred_element_type=fl_type) * score_scale
+    d_values = jnp.einsum("shqk,sqhd->skhd", probs.astype(bf_type), d_attn, preferred_element_type=fl_type)
+    d_mixed = jnp.stack((d_query, d_keys, d_values), axis=2).astype(bf_type)
+    d_mixed = d_mixed.reshape(seqs, full_rows, 3 * columns)
+
+    mixed_grad = outer_sum(all_tokens, d_mixed).astype(bf_type).reshape(count, own_rows, 3 * columns)
+    bias_mixed = row_total(d_mixed)
+    empty = jnp.zeros((width,), fl_type)
+    querybias_grad = lax.dynamic_update_slice_in_dim(empty, bias_mixed[:columns], seq_at * columns, 0)
+    valuebias_grad = lax.dynamic_update_slice_in_dim(empty, bias_mixed[2 * columns :], seq_at * columns, 0)
+    vector_grads = (
+        upbias_grad,
+        querybias_grad,
+        valuebias_grad,
+        outbias_grad,
+        attngain_grad,
+        attnshift_grad,
+        downbias_grad,
+        ffngain_grad,
+        ffnshift_grad,
+    )
+    small_grads = jnp.concatenate([item.reshape(count, -1) for item in vector_grads], axis=1)
+    small_size = small_grads.shape[1]
+    small_grads = jnp.pad(small_grads, ((0, 0), (0, small_room - small_size)))
+    small_grads = small_grads.reshape(count, SMALL_ROWS, 3 * columns).astype(bf_type)
+    arrived = exchange(jnp.concatenate((mixed_grad, small_grads), axis=1), BOTH, 0, 0).astype(fl_type)
+    qkv_shard = jnp.sum(arrived[:, :own_rows].reshape(dp_size, seq_size, own_rows, 3, columns), axis=0)
+    qkv_shard = jnp.transpose(qkv_shard, (2, 1, 0, 3)).reshape(3, own_rows, width)
+    small_sums = jnp.sum(arrived[:, own_rows:], axis=0).reshape(small_room)
+    vector_shards = []
+    at = 0
+    for item in vectors:
+        vector_shards.append(small_sums[at : at + item.shape[0]])
+        at += item.shape[0]
+
+    d_rows = exchange(d_mixed.reshape(seqs, full_rows, 3, columns), "seq", 1, 3)
+    d_rows = d_rows.reshape(seqs, rows, 3 * width)
+    grad_inputs = d_resid + project_back(d_rows, full_qkv)
+    return (
+        out_tokens,
+        grad_inputs.astype(bf_type),
+        qkv_shard[0],
+        qkv_shard[1],
+        qkv_shard[2],
+        outup_shard[:, :width],
+        outup_shard[:, width:],
+        down_shard.astype(fl_type),
+        vector_shards[1],
+        vector_shards[2],
+        vector_shards[3],
+        vector_shards[4],
+        vector_shards[5],
+        vector_shards[0],
+        vector_shards[6],
+        vector_shards[7],
+        vector_shards[8],
+    )
+
+
 def solution(mesh):
+    seq_size = mesh.shape["seq"]
+    by_heads = HEADS % seq_size == 0
+    body = functools.partial(local_heads, mesh.shape["dp"], seq_size) if by_heads else local_gathered
     return jax.shard_map(
-        local,
+        body,
         mesh=mesh,
         in_specs=(
             P("dp", "seq", None),

time: 1560 us -> 685 us (0.44)
  waiting for transfers between devices: 1160 us -> 466 us
  blocking collectives: 147 us -> 0 us
  matrix products: 139 us -> 95.1 us
  starting transfers between devices: 0.82 us -> 21.9 us
  local copies, waits for them, and re-layouts: 63.4 us -> 43.6 us
    unnamed x19 -> x6, waiting for transfers between devices: 435 us -> 1.43 us
    all_gather x10 -> x4, waiting for transfers between devices: 346 us -> 105 us  [the longest x1 56.5 us: local_heads(): full_down = lax.all_gather(w_down, BOTH, axis=0, tiled=True)]
    reduce_scatter x3 -> x2, waiting for transfers between devices: 383 us -> 185 us  [the longest x1 160 us: local_heads(): lax.psum_scatter(outup_grad, BOTH, scatter_dimension=0, tiled=True)]
    all_to_all x0 -> x5, waiting for transfers between devices: none -> 174 us  [exchange(): lax.all_to_all(values, axis, split_axis=split, concat_axis=join, tiled=True)]
    unnamed x2 -> x0, blocking collectives: 78.9 us -> none
    all_gather x3 -> x0, blocking collectives: 68.2 us -> none  [the longest x1 39.5 us: local(): lax.all_gather(b_up, ('dp', 'seq'), axis=0, tiled=True)]
    dot_general x7 -> x6, matrix products: 64 us -> 33.8 us  [the longest x1 10.8 us: local_heads(): jnp.einsum('sqhd,skhd->shqk', d_attn, values, preferred_element_type=fl_t...]
    unnamed x94 -> x62, local copies, waits for them, and re-layouts: 36.5 us -> 10.6 us
  transfers between devices with their start and end apart: 16 -> 11, of which waited for: 15 -> 10; matrix products, arithmetic and copies ran while one was open for 14% -> 24% of each run, Pallas kernels for 0% -> 0%
where the time goes in v1:
time: 685 us; the launch traced here: 676 us
  waiting for transfers between devices  466 us (68%)
  matrix products  95.1 us (14%)
  local copies, waits for them, and re-layouts  43.6 us (6%)
  other arithmetic  34.7 us (5%)
  starting transfers between devices  21.9 us (3%)
  between operations  15.1 us (2%)
    all_to_all x5, waiting for transfers between devices, exchange(): lax.all_to_all(values, axis, split_axis=split, concat_axis=join, tiled=True)  174 us
    reduce_scatter x1, waiting for transfers between devices, local_heads(): lax.psum_scatter(outup_grad, BOTH, scatter_dimension=0, tiled=True)  160 us
    all_gather x1, waiting for transfers between devices, local_heads(): full_down = lax.all_gather(w_down, BOTH, axis=0, tiled=True)  56.5 us
    all_gather x1, waiting for transfers between devices, local_heads(): lax.all_gather(jnp.concatenate((w_out, w_up), axis=1), BOTH, axis=0, tile...  47.6 us
    dot_general x4, matrix products, project_back(): jnp.einsum('sre,de->srd', grads, weight, preferred_element_type=jnp.float32)  26.5 us
    reduce_scatter x1, waiting for transfers between devices, local_heads(): lax.psum_scatter(downproj_grad.astype(bf_type), BOTH, scatter_dimension=0...  25.7 us
    all_to_all x5, starting transfers between devices, exchange(): lax.all_to_all(values, axis, split_axis=split, concat_axis=join, tiled=True)  21.7 us
    dot_general x4, matrix products, project(): jnp.einsum('srd,de->sre', values, weight, preferred_element_type=jnp.floa...  19.1 us
  transfers between devices with their start and end apart: 11, of which 10 were waited for; matrix products, arithmetic and copies ran while one was open for 24% of the time, Pallas kernels for 0%

profile of v1, /device:TPU:0, one launch (start us, length us, event | category | flops | bytes accessed | tf_op | source)
XLA Modules:
  0.0 676.4 jit_solution(891578208054972587)
XLA Ops:
  10.5 6.1 concatenate.28
  21.3 7.3 %all-to-all-start = ((bf16[32,40,384]{2,1,0:T(8,128)(2,1)}), bf16[32,40,384]{2,1,0:T(8,128)(2,1)S(1)}, u32[]{:S(2)}, u32[]{:S(2)}) async-start(bf16[32,40,384]{2,1,0:T(8,128)(2,1)} %bitcast.1), calls=%async_computation | async-start | bytes 1966080 | tf_op jit(solution)/shard_map/all_to_all | solution.py:280
  29.5 48.9 %all-to-all-done = bf16[32,40,384]{2,1,0:T(8,128)(2,1)S(1)} async-done(((bf16[32,40,384]{2,1,0:T(8,128)(2,1)}), bf16[32,40,384]{2,1,0:T(8,128)(2,1)S(1)}, u32[]{:S(2)}, u32[]{:S(2)}) %all-to-all-start) | async-done | bytes 983072 | tf_op jit(solution)/shard_map/all_to_all | solution.py:280
  80.3 4.1 add_convert_fusion.1
  87.8 3.5 fusion
  93.7 4.0 fusion.73
  98.8 3.5 all-to-all-start.1
  102.8 21.5 %all-to-all-done.1 = bf16[2,1024,128]{2,0,1:T(2,128)(2,1)S(1)} async-done(((bf16[2,1024,128]{2,0,1:T(2,128)(2,1)}), bf16[2,1024,128]{2,0,1:T(2,128)(2,1)S(1)}, u32[]{:S(2)}, u32[]{:S(2)}) %all-to-all-start.1) | async-done | bytes 524320 | tf_op jit(solution)/shard_map/all_to_all | solution.py:280
  124.9 47.6 %all-gather.7.cloned.1.call-done = bf16[1024,5120]{1,0:T(8,128)(2,1)} async-done(((bf16[32,5120]{1,0:T(8,128)(2,1)}), bf16[1024,5120]{1,0:T(8,128)(2,1)}) %all-gather.7.cloned.1.call-update) | async-done | bytes 10485776 | tf_op jit(solution)/shard_map/all_gather | solution.py:350
  175.4 6.7 fusion.56
  184.2 10.5 %multiply_convert_fusion.1 = (bf16[2,128,4096]{2,1,0:T(8,128)(2,1)S(1)}, f32[2,128,4096]{2,1,0:T(8,128)}) fusion(f32[2,128,4096]{2,1,0:T(8,128)S(1)} %get-tuple-element.67, u8[128,4096]{1,0:T(8,128)(4,1)S(1)} %get-tuple-element.18, u8[128,4096]{1,0:T(8,128)(4,1)S(1)} %get-tuple-element.17), kind=kLoop, calls=%fused_computation.33 | loop fusion | flops 73400320 | bytes 11534336 | tf_op jit(solution)/shard_map/convert_element_type | solution.py:378
  194.7 56.5 %all-gather.9.cloned.1.call-done = bf16[4096,1024]{1,0:T(8,128)(2,1)} async-done(((bf16[128,1024]{1,0:T(8,128)(2,1)}), bf16[4096,1024]{1,0:T(8,128)(2,1)}) %all-gather.9.cloned.1.call-update) | async-done | bytes 8388624 | tf_op jit(solution)/shard_map/all_gather | solution.py:352
  251.1 5.9 fusion.75
  260.2 5.6 bitcast_convert_fusion
  266.8 12.0 %fusion.76 = (bf16[4096]{0:T(1024)(128)(2,1)S(1)}, bf16[2,128,4096]{2,1,0:T(8,128)(2,1)S(1)}) fusion(f32[2,128,4096]{2,1,0:T(8,128)} %get-tuple-element.35, f32[2,128,4096]{2,1,0:T(8,128)} %copy-done.7, bf16[2,128,1024]{2,1,0:T(8,128)(2,1)S(1)} %copy-done.11, bf16[4096,1024]{1,0:T(8,128)(2,1)} %all-gather.9.cloned.1.call-done), kind=kOutput, calls=%fused_computation.142 | convolution fusion | flops 2163208192 | bytes 19406848 | tf_op jit(solution)/shard_map/sre,de->srd/dot_general | solution.py:32
  278.9 6.1 multiply_reduce_fusion
  291.5 4.0 bitcast_convert_fusion.1
  295.5 4.7 pad_maximum_fusion
  303.8 3.7 all-to-all-start.2
  308.0 22.0 %all-to-all-done.2 = bf16[2,128,1024]{1,0,2:T(2,128)(2,1)S(1)} async-done(((bf16[2,128,1024]{1,0,2:T(2,128)(2,1)}), bf16[2,128,1024]{1,0,2:T(2,128)(2,1)S(1)}, u32[]{:S(2)}, u32[]{:S(2)}) %all-to-all-start.2) | async-done | bytes 524320 | tf_op jit(solution)/shard_map/all_to_all | solution.py:280
  332.1 10.8 %multiply_convert_fusion = bf16[2,2,1024,1024]{2,3,1,0:T(8,128)(2,1)} fusion(f32[2,2,1024,1024]{2,3,1,0:T(8,128)} %copy-done, f32[2,2,1024]{2,1,0:T(2,128)S(1)} %bitcast.234, f32[2,2,1024]{2,1,0:T(2,128)S(1)} %log_add_fusion, pred[2,1024]{1,0:T(4,128)(4,1)S(1)} %iota_compare_fusion, bf16[2,1024,2,64]{1,3,2,0:T(8,128)(2,1)S(1)} %reshape.295, ...), kind=kOutput, calls=%fused_computation.2 | convolution fusion | flops 562036736 | bytes 26251264 | tf_op jit(solution)/shard_map/sqhd,skhd->shqk/dot_general | solution.py:408
  343.0 7.0 %convolution_multiply_fusion = bf16[2,2,64,1024]{3,2,1,0:T(8,128)(2,1)S(1)} fusion(bf16[2,2,1024,1024]{2,3,1,0:T(8,128)(2,1)} %multiply_convert_fusion, bf16[2,1024,3,2,64]{1,4,3,2,0:T(8,128)(2,1)S(1)} %bitcast.206), kind=kOutput, calls=%fused_computation.58 | convolution fusion | flops 537395200 | bytes 9437184 | tf_op jit(solution)/shard_map/shqk,sqhd->skhd/dot_general | solution.py:411
  350.0 5.0 convolution_multiply_fusion.1
  355.1 3.6 fusion.7
  360.0 4.0 fusion.43
  369.4 3.3 pad_maximum_fusion.1
  372.7 35.7 %all-to-all-done.4 = bf16[32,40,384]{2,1,0:T(8,128)(2,1)S(1)} async-done(((bf16[32,40,384]{2,1,0:T(8,128)(2,1)}), bf16[32,40,384]{2,1,0:T(8,128)(2,1)S(1)}, u32[]{:S(2)}, u32[]{:S(2)}) %all-to-all-start.4) | async-done | bytes 983072 | tf_op jit(solution)/shard_map/all_to_all | solution.py:280
  408.4 4.5 all-to-all-start.3
  423.2 45.7 %all-to-all-done.3 = bf16[2,1024,3,128]{3,0,2,1:T(2,128)(2,1)} async-done(((bf16[2,1024,3,128]{3,0,2,1:T(2,128)(2,1)}), bf16[2,1024,3,128]{3,0,2,1:T(2,128)(2,1)}, u32[]{:S(2)}, u32[]{:S(2)}) %all-to-all-start.3) | async-done | bytes 1572896 | tf_op jit(solution)/shard_map/all_to_all | solution.py:280
  473.0 6.0 fusion.45
  479.0 25.7 %reduce-scatter.5.cloned.1.call-done = bf16[128,1024]{1,0:T(8,128)(2,1)} async-done(((bf16[4096,1024]{1,0:T(8,128)(2,1)}), bf16[128,1024]{1,0:T(8,128)(2,1)}) %reduce-scatter.5.cloned.1.call-update) | async-done | bytes 262160 | tf_op jit(solution)/shard_map/reduce_scatter | solution.py:400
  506.4 159.6 %reduce-scatter.3.cloned.1.call-done = bf16[32,5120]{1,0:T(8,128)(2,1)} async-done(((bf16[1024,5120]{1,0:T(8,128)(2,1)}), bf16[32,5120]{1,0:T(8,128)(2,1)}) %reduce-scatter.3.cloned.1.call-update) | async-done | bytes 327696 | tf_op jit(solution)/shard_map/reduce_scatter | solution.py:402
  (176 shorter events, 66.2 us)
Async XLA Ops:
  7.2 21.5 %copy-start.20 = (bf16[32,1024]{1,0:T(8,128)(2,1)S(1)}, bf16[32,1024]{1,0:T(8,128)(2,1)}, u32[]{:S(2)}) copy-start(bf16[32,1024]{1,0:T(8,128)(2,1)} %param.22) | copy-start | bytes 196612
  7.2 21.5 %copy-start.21 = (bf16[32,1024]{1,0:T(8,128)(2,1)S(1)}, bf16[32,1024]{1,0:T(8,128)(2,1)}, u32[]{:S(2)}) copy-start(bf16[32,1024]{1,0:T(8,128)(2,1)} %param.21) | copy-start | bytes 196612
  7.2 21.5 %copy-start.22 = (bf16[32,1024]{1,0:T(8,128)(2,1)S(1)}, bf16[32,1024]{1,0:T(8,128)(2,1)}, u32[]{:S(2)}) copy-start(bf16[32,1024]{1,0:T(8,128)(2,1)} %param.20) | copy-start | bytes 196612
  7.2 22.2 %copy-start.23 = (s32[2]{0:T(128)S(1)}, s32[2]{0:T(128)}, u32[]{:S(2)}) copy-start(s32[2]{0:T(128)} %param.19) | copy-start | bytes 28
  7.2 73.1 %all-gather.5.cloned.1.call-start = ((), (), s32[]{:S(2)}) async-start(), calls=%async_computation.7 | async-start | bytes 4718592 | tf_op jit(solution)/shard_map/all_gather | solution.py:349
  8.0 164.5 %all-gather.7.cloned.1.call-start = ((), (), s32[]{:S(2)}) async-start(), calls=%async_computation.8 | async-start | bytes 10813440 | tf_op jit(solution)/shard_map/all_gather | solution.py:350
  9.7 241.4 %all-gather.9.cloned.1.call-start = ((), (), s32[]{:S(2)}) async-start(), calls=%async_computation.9 | async-start | bytes 8650752 | tf_op jit(solution)/shard_map/all_gather | solution.py:352
  21.3 57.2 %all-to-all-start = ((bf16[32,40,384]{2,1,0:T(8,128)(2,1)}), bf16[32,40,384]{2,1,0:T(8,128)(2,1)S(1)}, u32[]{:S(2)}, u32[]{:S(2)}) async-start(bf16[32,40,384]{2,1,0:T(8,128)(2,1)} %bitcast.1), calls=%async_computation | async-start | bytes 1966080 | tf_op jit(solution)/shard_map/all_to_all | solution.py:280
  28.6 444.4 %all-gather.11.cloned.1.call-start = ((), (), s32[]{:S(2)}) async-start(), calls=%async_computation.10 | async-start | bytes 6488064 | tf_op jit(solution)/shard_map/all_gather | solution.py:353
  84.4 6.8 %copy-start.8 = (bf16[384,2,1024]{2,0,1:T(8,128)(2,1)}, bf16[384,2,1024]{2,0,1:T(8,128)(2,1)S(1)}, u32[]{:S(2)}) copy-start(bf16[384,2,1024]{2,0,1:T(8,128)(2,1)S(1)} %add_convert_fusion.1) | copy-start | bytes 4718596
  87.8 5.9 copy-start
  97.7 74.8 %copy-start.19 = (bf16[2,128,1024]{2,1,0:T(8,128)(2,1)S(1)}, bf16[2,128,1024]{2,1,0:T(8,128)(2,1)}, u32[]{:S(2)}) copy-start(bf16[2,128,1024]{2,1,0:T(8,128)(2,1)} %param.18) | copy-start | bytes 1572868
  98.8 25.5 %all-to-all-start.1 = ((bf16[2,1024,128]{2,0,1:T(2,128)(2,1)}), bf16[2,1024,128]{2,0,1:T(2,128)(2,1)S(1)}, u32[]{:S(2)}, u32[]{:S(2)}) async-start(bf16[2,1024,128]{2,0,1:T(2,128)(2,1)} %copy.126), calls=%async_computation.1 | async-start | bytes 1048576 | tf_op jit(solution)/shard_map/all_to_all | solution.py:280
  102.3 402.4 %reduce-scatter.5.cloned.1.call-start = ((), (), s32[]{:S(2)}) async-start(), calls=%async_computation.12 | async-start | bytes 8650752 | tf_op jit(solution)/shard_map/reduce_scatter | solution.py:400
  124.9 57.2 %copy-start.14 = (bf16[2,128,1024]{2,1,0:T(8,128)(2,1)}, bf16[2,128,1024]{2,1,0:T(8,128)(2,1)S(1)}, u32[]{:S(2)}) copy-start(bf16[2,128,1024]{2,1,0:T(8,128)(2,1)S(1)} %all_to_all.45) | copy-start | bytes 1572868
  175.4 6.7 copy-start.17
  251.1 5.9 copy-start.3
  265.8 400.2 %reduce-scatter.3.cloned.1.call-start = ((), (), s32[]{:S(2)}) async-start(), calls=%async_computation.11 | async-start | bytes 10813440 | tf_op jit(solution)/shard_map/reduce_scatter | solution.py:402
  266.8 12.0 %copy-start.2 = (f32[2,128,1024]{2,1,0:T(8,128)S(1)}, f32[2,128,1024]{2,1,0:T(8,128)}, u32[]{:S(2)}) copy-start(f32[2,128,1024]{2,1,0:T(8,128)} %copy-done.1) | copy-start | bytes 3145732
  266.8 12.0 %copy-start.4 = (bf16[2,128,1024]{2,1,0:T(8,128)(2,1)S(1)}, bf16[2,128,1024]{2,1,0:T(8,128)(2,1)}, u32[]{:S(2)}) copy-start(bf16[2,128,1024]{2,1,0:T(8,128)(2,1)} %param.35) | copy-start | bytes 1572868
  278.8 6.1 copy-start.16
  286.4 5.2 copy-start.18
  300.2 31.9 %copy-start.9 = (bf16[384,2,1024]{2,0,1:T(8,128)(2,1)S(1)}, bf16[384,2,1024]{2,0,1:T(8,128)(2,1)}, u32[]{:S(2)}) copy-start(bf16[384,2,1024]{2,0,1:T(8,128)(2,1)} %copy-done.8) | copy-start | bytes 4718596
  303.8 26.1 %all-to-all-start.2 = ((bf16[2,128,1024]{1,0,2:T(2,128)(2,1)}), bf16[2,128,1024]{1,0,2:T(2,128)(2,1)S(1)}, u32[]{:S(2)}, u32[]{:S(2)}) async-start(bf16[2,128,1024]{1,0,2:T(2,128)(2,1)} %copy.128), calls=%async_computation.2 | async-start | bytes 1048576 | tf_op jit(solution)/shard_map/all_to_all | solution.py:280
  330.5 12.5 %copy-start.12 = (bf16[2,1024,2,64]{1,3,2,0:T(8,128)(2,1)}, bf16[2,1024,2,64]{1,3,2,0:T(8,128)(2,1)S(1)}, u32[]{:S(2)}) copy-start(bf16[2,1024,2,64]{1,3,2,0:T(8,128)(2,1)S(1)} %reshape.295) | copy-start | bytes 1572868
  332.1 22.9 %slice-start = ((s8[16777216]{0:T(1024)(128)(4,1)}), s8[4194304]{0:T(1024)(128)(4,1)S(1)}, s32[]{:S(2)}) async-start(s8[16777216]{0:T(1024)(128)(4,1)} %bitcast.195), calls=%async_computation.13 | async-start | bytes 8388608
  332.1 22.9 %slice-start.1 = ((s8[16777216]{0:T(1024)(128)(4,1)}), s8[4194304]{0:T(1024)(128)(4,1)S(1)}, s32[]{:S(2)}) async-start(s8[16777216]{0:T(1024)(128)(4,1)} %bitcast.195), calls=%async_computation.14 | async-start | bytes 8388608
  332.1 22.9 %slice-start.2 = ((s8[16777216]{0:T(1024)(128)(4,1)}), s8[4194304]{0:T(1024)(128)(4,1)S(1)}, s32[]{:S(2)}) async-start(s8[16777216]{0:T(1024)(128)(4,1)} %bitcast.195), calls=%async_computation.15 | async-start | bytes 8388608
  343.0 12.1 %slice-start.3 = ((s8[16777216]{0:T(1024)(128)(4,1)}), s8[4194304]{0:T(1024)(128)(4,1)S(1)}, s32[]{:S(2)}) async-start(s8[16777216]{0:T(1024)(128)(4,1)} %bitcast.195), calls=%async_computation.16 | async-start | bytes 8388608
  365.4 43.0 %all-to-all-start.4 = ((bf16[32,40,384]{2,1,0:T(8,128)(2,1)}), bf16[32,40,384]{2,1,0:T(8,128)(2,1)S(1)}, u32[]{:S(2)}, u32[]{:S(2)}) async-start(bf16[32,40,384]{2,1,0:T(8,128)(2,1)} %pad_maximum_fusion.2), calls=%async_computation.4 | async-start | bytes 1966080 | tf_op jit(solution)/shard_map/all_to_all | solution.py:280
  408.4 60.6 %all-to-all-start.3 = ((bf16[2,1024,3,128]{3,0,2,1:T(2,128)(2,1)}), bf16[2,1024,3,128]{3,0,2,1:T(2,128)(2,1)}, u32[]{:S(2)}, u32[]{:S(2)}) async-start(bf16[2,1024,3,128]{3,0,2,1:T(2,128)(2,1)} %pad_maximum_fusion.1), calls=%async_computation.3 | async-start | bytes 3145728 | tf_op jit(solution)/shard_map/all_to_all | solution.py:280
  421.3 51.7 %copy-start.6 = (f32[2,128,1024]{2,1,0:T(8,128)S(1)}, f32[2,128,1024]{2,1,0:T(8,128)}, u32[]{:S(2)}) copy-start(f32[2,128,1024]{2,1,0:T(8,128)} %copy-done.5) | copy-start | bytes 3145732
  (7 other events, 13.4 us)
Sparse Core Ops, SparseCore 0:
  9.6 70.6 all-gather.4
  83.8 88.6 all-gather.6
  175.5 75.5 all-gather.8
  254.0 76.5 all-gather.10
  332.8 171.8 reduce-scatter.4
  506.8 159.1 reduce-scatter.2
